TPU v7x, 32 devices: a whole 2x2x4 slice. The times are simulated.
32 devices in a mesh: imp: 8 (over z, y), camp: 4 (over x, core).
Axes of the slice: x: 2, y: 2, z: 4, core: 2. Of those that a mesh axis runs over, the one named last changes fastest.
Arguments:
- imp_emb: bfloat16 [16384, 256], P(('imp', 'camp')), may hold values from -512 to 512
- imp_cost: bfloat16 [16384], P(('imp', 'camp')), may hold values from 0.099609375 to 1
- camp_emb: bfloat16 [4096, 256], P(('camp', 'imp')), may hold values from -6 to 6
- prices: bfloat16 [4096], P(('camp', 'imp')), may hold values from -5 to 5
- spend_limits: float32 [4096], P(('camp', 'imp')), may hold values from 3 to 32
- block_lists: int32 [128, 4, 8], P('imp', 'camp'), may hold values from 0 to 7, as said below
- block_counts: int32 [128, 4], P('imp', 'camp'), may hold values from 1 to 8, as said below
Outputs:
- new_prices: float32 [4096], P(('camp', 'imp'))
- row_logz: float32 [16384], P('imp')
Inputs may be any that keep to these rules, and one draw needn't show every extreme that they name: `block_lists`: entries of a list of one tile and owner are distinct block numbers of that owner; slots past the count hold block numbers too, which are ignored. `block_counts`: tile 0 uses all 8 slots of every owner.
All inputs are finite; a program needn't handle non-finite values.
Results may differ from a plain program's by a relative error of at most 0.0003.
Values may be sent and summed in bfloat16 or wider, within the bound.
A program may use at most 64 MiB of HBM per device.

v0:
```python
import jax
import jax.numpy as jnp
from jax import lax
from jax.sharding import PartitionSpec as P

D = 256
BLOCK = 128
SLOTS = 8
GROUP = 4


def merged(array, axis, combine):
    everything = jax.tree.map(lambda part: lax.all_gather(part, axis), array)
    initial = jax.tree.map(lambda part: part[0], everything)

    def step(k, so_far):
        return combine(so_far, jax.tree.map(lambda part: part[k], everything))

    return lax.fori_loop(1, lax.axis_size(axis), step, initial)


def local(imp_emb, imp_cost, camp_emb, prices, spend_limits, block_lists, block_counts):
    scale = 3.0 / jnp.sqrt(jnp.float32(D))
    emb_rows, cost_rows = (
        lax.all_gather(imp_emb, "camp", axis=0, tiled=True),
        lax.all_gather(imp_cost, "camp", axis=0, tiled=True),
    )
    camp_all, price_all = (
        lax.all_gather(camp_emb, "imp", axis=0, tiled=True),
        lax.all_gather(prices, "imp", axis=0, tiled=True),
    )
    own_count = camp_all.shape[0] // BLOCK
    camp_table = camp_all.reshape(own_count, BLOCK, D)
    price_table = price_all.astype(jnp.float32).reshape(own_count, BLOCK)
    lists = block_lists[:, 0, :]
    counts = block_counts[:, 0]
    tiles = lists.shape[0]
    turns = tiles // GROUP
    emb_groups = emb_rows.reshape(turns, GROUP, BLOCK, D)
    cost_groups = cost_rows.astype(jnp.float32).reshape(turns, GROUP, BLOCK)
    list_groups = lists.reshape(turns, GROUP, SLOTS)
    count_groups = counts.reshape(turns, GROUP)

    def scores_of(emb, ids, cnt):
        chosen = camp_table[ids]
        chosen_price = price_table[ids]
        raw = jnp.einsum("gbd,gscd->gbsc", emb, chosen, preferred_element_type=jnp.float32)
        logits = raw * scale - chosen_price[:, None, :, :]
        live = (jnp.arange(SLOTS, dtype=jnp.int32)[None, :] < cnt[:, None])[:, None, :, None]
        return (logits, live)

    def local_both(items):
        emb, ids, cnt = items
        logits, live = scores_of(emb, ids, cnt)
        top_here = jnp.max(jnp.where(live, logits, -jnp.inf), axis=(2, 3))
        expo = jnp.exp(jnp.where(live, logits - top_here[:, :, None, None], -jnp.inf))
        return (top_here, jnp.sum(expo, axis=(2, 3)))

    tops_here, totals_here = lax.map(local_both, (emb_groups, list_groups, count_groups))

    def combine(first, second):
        larger = jnp.maximum(first[0], second[0])
        summed = first[1] * jnp.exp(first[0] - larger) + second[1] * jnp.exp(second[0] - larger)
        return (larger, summed)

    top, total = merged((tops_here, totals_here), "camp", combine)
    row_logz = (top + jnp.log(total)).reshape(tiles * BLOCK)
    block_index = jnp.arange(own_count, dtype=jnp.int32)

    def accumulate(spend, items):
        emb, ids, cnt, cost, top_now, total_now = items
        logits, live = scores_of(emb, ids, cnt)
        expo = jnp.exp(jnp.where(live, logits - top_now[:, :, None, None], -jnp.inf))
        weight = expo / total_now[:, :, None, None]
        contrib = jnp.sum(weight * cost[:, :, None, None], axis=1)
        slot_live = jnp.arange(SLOTS, dtype=jnp.int32)[None, :] < cnt[:, None]
        onehot = ((ids[:, :, None] == block_index[None, None, :]) & slot_live[:, :, None]).astype(
            jnp.float32
        )
        added = jnp.einsum("gso,gsc->oc", onehot, contrib, precision=lax.Precision.HIGHEST)
        return (spend + added, None)

    spend_zero = jnp.zeros((own_count, BLOCK), jnp.float32)
    spend, unused = lax.scan(
        accumulate, spend_zero, (emb_groups, list_groups, count_groups, cost_groups, top, total)
    )
    spend = spend.reshape(own_count * BLOCK)
    width = prices.shape[0]
    whole = lax.psum(spend, "imp")
    mine = lax.dynamic_slice_in_dim(whole, lax.axis_index("imp") * width, width)
    new_prices = prices.astype(jnp.float32) + 2.0 * (mine - spend_limits) / (mine + spend_limits)
    return (new_prices, row_logz)


def solution(mesh):
    return jax.shard_map(
        local,
        mesh=mesh,
        in_specs=(
            P(("imp", "camp"), None),
            P(("imp", "camp")),
            P(("camp", "imp"), None),
            P(("camp", "imp")),
            P(("camp", "imp")),
            P("imp", "camp", None),
            P("imp", "camp"),
        ),
        out_specs=(P(("camp", "imp")), P("imp")),
        check_vma=False,
    )
```

profile of v0, /device:TPU:0, one launch (start us, length us, event | category | flops | bytes accessed | tf_op | source)
XLA Modules:
  0.0 137.3 jit_solution(15288913521605371296)
XLA Ops:
  7.2 0.7 all-gather.6.cloned.1.call-update
  7.9 0.8 copy.12
  8.7 22.5 %all-gather.2 = bf16[8,1,128]{2,1,0:T(2,128)(2,1)S(1)} all-gather(bf16[1,1,128]{2,1,0:T(2,128)(2,1)} %bitcast.128), channel_id=1, replica_groups=mesh['imp'=8,'camp'=4] {'imp'}, dimensions={0}, use_global_device_ids=true | all-gather | bytes 2304 | tf_op jit(solution)/shard_map/all_gather | solution.py:30
  31.7 1.2 reduce.3
  33.0 0.7 reshape.223
  33.7 5.2 %all-gather.3 = bf16[4,1,512]{2,1,0:T(2,128)(2,1)S(1)} all-gather(bf16[1,1,512]{2,1,0:T(2,128)(2,1)S(1)} %reshape.223), channel_id=1, replica_groups=mesh['imp'=8,'camp'=4] {'camp'}, dimensions={0}, use_global_device_ids=true | all-gather | bytes 5120 | tf_op jit(solution)/shard_map/all_gather | solution.py:26
  38.9 31.4 %all_gather.25 = bf16[1024,256]{1,0:T(8,128)(2,1)S(1)} all-gather(bf16[128,256]{1,0:T(8,128)(2,1)} %param.15), channel_id=1, replica_groups=mesh['imp'=8,'camp'=4] {'imp'}, dimensions={0}, use_global_device_ids=true | all-gather | bytes 589824 | tf_op jit(solution)/shard_map/all_gather | solution.py:29
  70.3 16.5 %while.40 = (s32[]{:T(128)}, f32[4,4,128]{2,1,0:T(4,128)S(1)}, f32[4,4,128]{2,1,0:T(4,128)S(1)}, s32[4,4]{1,0:T(4,128)S(1)}, bf16[4,4,128,256]{3,2,1,0:T(8,128)(...) while((s32[]{:T(128)}, f32[4,4,128]{2,1,0:T(4,128)S(1)}, ...), condition=%wide.region_3.4_spmd, body=%wide.region_0.3_spmd.sunk | while | flops 273154176 | bytes 10833529 | solution.py:59
  71.0 0.7 gather_fusion.1
  71.7 1.9 %select_reduce_fusion.2 = (f32[4,128]{1,0:T(4,128)S(1)}, f32[4,128,8,128]{1,3,2,0:T(8,128)S(1)}) fusion(f32[4,8,128]{2,1,0:T(8,128)S(1)} %bitcast.117, pred[4,8]{1,0:T(4,128)(4,1)S(1)} %iota_compare_fusion.5, bf16[4,8,128,256]{3,2,1,0:T(8,128)(2,1)S(1)} %bitcast.116, bf16[4,4,128,256]{3,2,1,0:T(8,128)(2,1)} %get-tuple-element.508, ...), kind=kOutput, calls=%fused_computation.11.clone.1 | convolution fusion | flops 270532096 | bytes 4475424 | tf_op jit(solution)/shard_map/while/body/eval_jaxpr/gbd,gscd->gbsc/dot_general | solution.py:47
  73.6 0.8 exponential_reduce_fusion.2
  75.1 0.7 gather_fusion.1
  75.9 1.9 %select_reduce_fusion.2 = (f32[4,128]{1,0:T(4,128)S(1)}, f32[4,128,8,128]{1,3,2,0:T(8,128)S(1)}) fusion(f32[4,8,128]{2,1,0:T(8,128)S(1)} %bitcast.117, pred[4,8]{1,0:T(4,128)(4,1)S(1)} %iota_compare_fusion.5, bf16[4,8,128,256]{3,2,1,0:T(8,128)(2,1)S(1)} %bitcast.116, bf16[4,4,128,256]{3,2,1,0:T(8,128)(2,1)} %get-tuple-element.508, ...), kind=kOutput, calls=%fused_computation.11.clone.1 | convolution fusion | flops 270532096 | bytes 4475424 | tf_op jit(solution)/shard_map/while/body/eval_jaxpr/gbd,gscd->gbsc/dot_general | solution.py:47
  77.7 0.8 exponential_reduce_fusion.2
  79.2 0.7 gather_fusion.1
  80.0 1.9 %select_reduce_fusion.2 = (f32[4,128]{1,0:T(4,128)S(1)}, f32[4,128,8,128]{1,3,2,0:T(8,128)S(1)}) fusion(f32[4,8,128]{2,1,0:T(8,128)S(1)} %bitcast.117, pred[4,8]{1,0:T(4,128)(4,1)S(1)} %iota_compare_fusion.5, bf16[4,8,128,256]{3,2,1,0:T(8,128)(2,1)S(1)} %bitcast.116, bf16[4,4,128,256]{3,2,1,0:T(8,128)(2,1)} %get-tuple-element.508, ...), kind=kOutput, calls=%fused_computation.11.clone.1 | convolution fusion | flops 270532096 | bytes 4475424 | tf_op jit(solution)/shard_map/while/body/eval_jaxpr/gbd,gscd->gbsc/dot_general | solution.py:47
  81.9 0.8 exponential_reduce_fusion.2
  83.4 0.7 gather_fusion.1
  84.1 1.9 %select_reduce_fusion.2 = (f32[4,128]{1,0:T(4,128)S(1)}, f32[4,128,8,128]{1,3,2,0:T(8,128)S(1)}) fusion(f32[4,8,128]{2,1,0:T(8,128)S(1)} %bitcast.117, pred[4,8]{1,0:T(4,128)(4,1)S(1)} %iota_compare_fusion.5, bf16[4,8,128,256]{3,2,1,0:T(8,128)(2,1)S(1)} %bitcast.116, bf16[4,4,128,256]{3,2,1,0:T(8,128)(2,1)} %get-tuple-element.508, ...), kind=kOutput, calls=%fused_computation.11.clone.1 | convolution fusion | flops 270532096 | bytes 4475424 | tf_op jit(solution)/shard_map/while/body/eval_jaxpr/gbd,gscd->gbsc/dot_general | solution.py:47
  86.0 0.8 exponential_reduce_fusion.2
  86.8 5.2 %all-gather = f32[16,4,128]{2,1,0:T(4,128)S(1)} all-gather(f32[4,4,128]{2,1,0:T(4,128)S(1)} %get-tuple-element.235), channel_id=2, replica_groups=mesh['imp'=8,'camp'=4] {'camp'}, dimensions={0}, use_global_device_ids=true | all-gather | bytes 40960 | tf_op jit(solution)/shard_map/all_gather | solution.py:13
  92.0 5.2 %all-gather.1 = f32[16,4,128]{2,1,0:T(4,128)S(1)} all-gather(f32[4,4,128]{2,1,0:T(4,128)S(1)} %get-tuple-element.236), channel_id=3, replica_groups=mesh['imp'=8,'camp'=4] {'camp'}, dimensions={0}, use_global_device_ids=true | all-gather | bytes 40960 | tf_op jit(solution)/shard_map/all_gather | solution.py:13
  97.3 14.7 %while.42 = (s32[]{:T(128)}, f32[8,128]{1,0:T(8,128)S(1)}, s32[4,4,8]{2,1,0:T(4,128)S(1)}, s32[4,4]{1,0:T(4,128)S(1)}, bf16[4,4,128,256]{3,2,1,0:T(8,128)(2,1)},...) while((s32[]{:T(128)}, f32[8,128]{1,0:T(8,128)S(1)}, ...), condition=%wide.region_8.9_spmd.clone, body=%wide.region_6.8_spmd.clone.sunk | while | flops 272498304 | bytes 6668323 | solution.py:84
  97.5 0.7 gather_fusion.2
  98.8 2.0 %multiply_reduce_fusion.2 = f32[4,8,128]{2,1,0:T(8,128)S(1)} fusion(bf16[4,8,128,256]{3,2,1,0:T(8,128)(2,1)S(1)} %bitcast.115, f32[4,128]{1,0:T(4,128)S(1)} %get-tuple-element.484, f32[4,128]{1,0:T(4,128)S(1)} %get-tuple-element.485, f32[4,128]{1,0:T(4,128)S(1)} %dynamic-slice_bitcast_fusion.8, f32[4,8,128]{2,1,0:T(8,128)S(1)} %bitcast.121, ...), kind=kOutput, calls=%fused_computation.24.clone.1 | convolution fusion | flops 272101376 | bytes 2398752 | tf_op jit(solution)/shard_map/while/body/eval_jaxpr/gbd,gscd->gbsc/dot_general | solution.py:47
  101.1 0.7 gather_fusion.2
  102.5 2.0 %multiply_reduce_fusion.2 = f32[4,8,128]{2,1,0:T(8,128)S(1)} fusion(bf16[4,8,128,256]{3,2,1,0:T(8,128)(2,1)S(1)} %bitcast.115, f32[4,128]{1,0:T(4,128)S(1)} %get-tuple-element.484, f32[4,128]{1,0:T(4,128)S(1)} %get-tuple-element.485, f32[4,128]{1,0:T(4,128)S(1)} %dynamic-slice_bitcast_fusion.8, f32[4,8,128]{2,1,0:T(8,128)S(1)} %bitcast.121, ...), kind=kOutput, calls=%fused_computation.24.clone.1 | convolution fusion | flops 272101376 | bytes 2398752 | tf_op jit(solution)/shard_map/while/body/eval_jaxpr/gbd,gscd->gbsc/dot_general | solution.py:47
  104.8 0.7 gather_fusion.2
  106.2 2.0 %multiply_reduce_fusion.2 = f32[4,8,128]{2,1,0:T(8,128)S(1)} fusion(bf16[4,8,128,256]{3,2,1,0:T(8,128)(2,1)S(1)} %bitcast.115, f32[4,128]{1,0:T(4,128)S(1)} %get-tuple-element.484, f32[4,128]{1,0:T(4,128)S(1)} %get-tuple-element.485, f32[4,128]{1,0:T(4,128)S(1)} %dynamic-slice_bitcast_fusion.8, f32[4,8,128]{2,1,0:T(8,128)S(1)} %bitcast.121, ...), kind=kOutput, calls=%fused_computation.24.clone.1 | convolution fusion | flops 272101376 | bytes 2398752 | tf_op jit(solution)/shard_map/while/body/eval_jaxpr/gbd,gscd->gbsc/dot_general | solution.py:47
  108.5 0.7 gather_fusion.2
  109.9 2.0 %multiply_reduce_fusion.2 = f32[4,8,128]{2,1,0:T(8,128)S(1)} fusion(bf16[4,8,128,256]{3,2,1,0:T(8,128)(2,1)S(1)} %bitcast.115, f32[4,128]{1,0:T(4,128)S(1)} %get-tuple-element.484, f32[4,128]{1,0:T(4,128)S(1)} %get-tuple-element.485, f32[4,128]{1,0:T(4,128)S(1)} %dynamic-slice_bitcast_fusion.8, f32[4,8,128]{2,1,0:T(8,128)S(1)} %bitcast.121, ...), kind=kOutput, calls=%fused_computation.24.clone.1 | convolution fusion | flops 272101376 | bytes 2398752 | tf_op jit(solution)/shard_map/while/body/eval_jaxpr/gbd,gscd->gbsc/dot_general | solution.py:47
  112.1 17.2 %psum.7 = f32[1024]{0:T(1024)S(1)} all-reduce(f32[1024]{0:T(1024)S(1)} %bitcast.125), channel_id=1, replica_groups=mesh['imp'=8,'camp'=4] {'imp'}, use_global_device_ids=true, to_apply=%region_9.10 | all-reduce | flops 1024 | bytes 8192 | tf_op jit(solution)/shard_map/psum | solution.py:89
  (89 shorter events, 9.1 us)
Async XLA Ops:
  7.2 63.1 %all-gather.6.cloned.1.call-start = ((), (), s32[]{:S(2)}) async-start(), calls=%async_computation | async-start | bytes 1310720 | tf_op jit(solution)/shard_map/all_gather | solution.py:25
  97.3 32.6 %copy-start = (bf16[128]{0:T(256)(128)(2,1)S(1)}, bf16[128]{0:T(256)(128)(2,1)}, u32[]{:S(2)}) copy-start(bf16[128]{0:T(256)(128)(2,1)} %param.16) | copy-start | bytes 772
  97.3 32.6 %copy-start.1 = (f32[128]{0:T(128)S(1)}, f32[128]{0:T(128)}, u32[]{:S(2)}) copy-start(f32[128]{0:T(128)} %param.17) | copy-start | bytes 1540
Sparse Core Ops, SparseCore 0:
  9.5 19.4 all-gather.5
where the time goes:
time: 138 us; the launch traced here: 137 us
  blocking collectives  86.6 us (63%)
  matrix products  16 us (12%)
  between operations  14.1 us (10%)
  local copies, waits for them, and re-layouts  13 us (9%)
  other arithmetic  6.35 us (5%)
    all_gather x1, blocking collectives, local(): lax.all_gather(camp_emb, 'imp', axis=0, tiled=True)  31.4 us
    all_gather x1, blocking collectives, local(): lax.all_gather(prices, 'imp', axis=0, tiled=True)  22.5 us
    psum x1, blocking collectives, local(): whole = lax.psum(spend, 'imp')  17.2 us
    dot_general x8, matrix products, scores_of(): jnp.einsum('gbd,gscd->gbsc', emb, chosen, preferred_element_type=jnp.floa...  15.3 us
    all_gather x2, blocking collectives, merged(): everything = jax.tree.map(lambda part: lax.all_gather(part, axis), array)  10.4 us
    gather x8, local copies, waits for them, and re-layouts, scores_of(): chosen = camp_table[ids]  5.48 us
    all_gather x1, blocking collectives, local(): lax.all_gather(imp_cost, 'camp', axis=0, tiled=True)  5.18 us
    gather x8, local copies, waits for them, and re-layouts, scores_of(): chosen_price = price_table[ids]  4.59 us
  transfers between devices with their start and end apart: 1, of which 0 were waited for; matrix products, arithmetic and copies ran while one was open for 2% of the time, Pallas kernels for 0%

commit v1 on v0

--- a/solution.py
+++ b/solution.py
@@ -7,6 +7,27 @@
 BLOCK = 128
 SLOTS = 8
 GROUP = 4
+
+
+def in_order(blocks, dim):
+    lengths = list(blocks.shape[1:])
+    lengths[dim] *= blocks.shape[0]
+    return jnp.moveaxis(blocks, 0, dim).reshape(lengths)
+
+
+def collected_by_bits(x, axis):
+    size, place = (lax.axis_size(axis), lax.axis_index(axis))
+    pieces, bit = (x[None], 1)
+    while bit < size:
+        theirs = lax.ppermute(pieces, axis, [(i, i ^ bit) for i in range(size)])
+        low = place & bit == 0
+        pieces = jnp.concatenate([jnp.where(low, pieces, theirs), jnp.where(low, theirs, pieces)])
+        bit *= 2
+    return pieces
+
+
+def doubled_up(x, axis, dim):
+    return in_order(collected_by_bits(x, axis), dim)
 
 
 def merged(array, axis, combine):
@@ -27,7 +48,7 @@
     )
     camp_all, price_all = (
         lax.all_gather(camp_emb, "imp", axis=0, tiled=True),
-        lax.all_gather(prices, "imp", axis=0, tiled=True),
+        doubled_up(prices, "imp", 0),
     )
     own_count = camp_all.shape[0] // BLOCK
     camp_table = camp_all.reshape(own_count, BLOCK, D)

time: 138 us -> 125 us (0.906)
  blocking collectives: 86.6 us -> 68.1 us
  starting transfers between devices: 0.04 us -> 4.33 us
    all_gather x1 -> x0, blocking collectives: 22.5 us -> none  [local(): lax.all_gather(prices, 'imp', axis=0, tiled=True)]
    ppermute x0 -> x3, starting transfers between devices: none -> 4.29 us  [collected_by_bits(): theirs = lax.ppermute(pieces, axis, [(i, i ^ bit) for i in range(size)])]
    psum x1, blocking collectives: 17.2 us -> 20.3 us  [local(): whole = lax.psum(spend, 'imp')]
  transfers between devices with their start and end apart: 1 -> 4, of which waited for: 0 -> 1; matrix products, arithmetic and copies ran while one was open for 2% -> 3% of each run, Pallas kernels for 0% -> 0%
where the time goes in v1:
time: 125 us
  blocking collectives  68.1 us (54%)
  matrix products  16.1 us (13%)
  between operations  14.1 us (11%)
  local copies, waits for them, and re-layouts  13.1 us (10%)
  other arithmetic  7.16 us (6%)
  starting transfers between devices  4.33 us (3%)
  waiting for transfers between devices  1.29 us (1%)
    all_gather x1, blocking collectives, local(): lax.all_gather(camp_emb, 'imp', axis=0, tiled=True)  32.2 us
    psum x1, blocking collectives, local(): whole = lax.psum(spend, 'imp')  20.3 us
    dot_general x8, matrix products, scores_of(): jnp.einsum('gbd,gscd->gbsc', emb, chosen, preferred_element_type=jnp.floa...  15.3 us
    all_gather x2, blocking collectives, merged(): everything = jax.tree.map(lambda part: lax.all_gather(part, axis), array)  10.4 us
    gather x8, local copies, waits for them, and re-layouts, scores_of(): chosen = camp_table[ids]  5.48 us
    all_gather x1, blocking collectives, local(): lax.all_gather(imp_cost, 'camp', axis=0, tiled=True)  5.19 us
    gather x8, local copies, waits for them, and re-layouts, scores_of(): chosen_price = price_table[ids]  4.59 us
    ppermute x3, starting transfers between devices, collected_by_bits(): theirs = lax.ppermute(pieces, axis, [(i, i ^ bit) for i in range(size)])  4.29 us
  transfers between devices with their start and end apart: 4, of which 1 were waited for; matrix products, arithmetic and copies ran while one was open for 3% of the time, Pallas kernels for 0%

profile of v1, /device:TPU:0, one launch (start us, length us, event | category | flops | bytes accessed | tf_op | source)
XLA Modules:
  0.0 124.6 jit_solution(13219708661366072794)
XLA Ops:
  7.2 0.7 all-gather.5.cloned.1.call-update
  7.9 3.1 %collective-permute-start = (bf16[1,128]{1,0:T(2,128)(2,1)}, bf16[1,128]{1,0:T(2,128)(2,1)S(1)}, u32[]{:S(2)}, u32[]{:S(2)}) collective-permute-start(bf16[1,128]{1,0:T(2,128)(2,1)} %bitcast.128), channel_id=1, source_target_pairs={{0,4},{4,0},{8,12},{12,8},{16,20},{20,16},{24,28},{28,24},{1,5},{5... | collective-permute-start | bytes 776 | tf_op jit(solution)/shard_map/ppermute | solution.py:22
  11.0 32.2 %all_gather.22 = bf16[1024,256]{1,0:T(8,128)(2,1)S(1)} all-gather(bf16[128,256]{1,0:T(8,128)(2,1)} %param.15), channel_id=1, replica_groups=mesh['imp'=8,'camp'=4] {'imp'}, dimensions={0}, use_global_device_ids=true | all-gather | bytes 589824 | tf_op jit(solution)/shard_map/all_gather | solution.py:50
  43.1 0.7 reshape.213
  44.5 5.2 %all-gather.2 = bf16[4,1,512]{2,1,0:T(2,128)(2,1)S(1)} all-gather(bf16[1,1,512]{2,1,0:T(2,128)(2,1)S(1)} %reshape.213), channel_id=1, replica_groups=mesh['imp'=8,'camp'=4] {'camp'}, dimensions={0}, use_global_device_ids=true | all-gather | bytes 5120 | tf_op jit(solution)/shard_map/all_gather | solution.py:47
  49.8 1.2 collective-permute-start.2
  50.9 0.8 copy.12
  52.3 1.4 %reduce.3 = s32[16]{0:T(128)S(1)} reduce(s32[16,1]{0,1:T(1,128)} %param.19, s32[]{:T(128)} %broadcast.122), dimensions={1}, to_apply=%param.19.reduce_sub_computation.3 | reduce | bytes 132 | tf_op args[6]
  54.4 16.5 %while.40 = (s32[]{:T(128)}, f32[4,4,128]{2,1,0:T(4,128)S(1)}, f32[4,4,128]{2,1,0:T(4,128)S(1)}, s32[4,4]{1,0:T(4,128)S(1)}, bf16[4,4,128,256]{3,2,1,0:T(8,128)(...) while((s32[]{:T(128)}, f32[4,4,128]{2,1,0:T(4,128)S(1)}, ...), condition=%wide.region_3.4_spmd, body=%wide.region_0.3_spmd.sunk | while | flops 273154176 | bytes 10833529 | solution.py:80
  55.1 0.7 gather_fusion.1
  55.8 1.9 %select_reduce_fusion.2 = (f32[4,128]{1,0:T(4,128)S(1)}, f32[4,128,8,128]{1,3,2,0:T(8,128)S(1)}) fusion(f32[4,8,128]{2,1,0:T(8,128)S(1)} %bitcast.117, pred[4,8]{1,0:T(4,128)(4,1)S(1)} %iota_compare_fusion.5, bf16[4,8,128,256]{3,2,1,0:T(8,128)(2,1)S(1)} %bitcast.116, bf16[4,4,128,256]{3,2,1,0:T(8,128)(2,1)} %get-tuple-element.514, ...), kind=kOutput, calls=%fused_computation.11.clone.1 | convolution fusion | flops 270532096 | bytes 4475424 | tf_op jit(solution)/shard_map/while/body/eval_jaxpr/gbd,gscd->gbsc/dot_general | solution.py:68
  57.7 0.8 exponential_reduce_fusion.2
  59.2 0.7 gather_fusion.1
  60.0 1.9 %select_reduce_fusion.2 = (f32[4,128]{1,0:T(4,128)S(1)}, f32[4,128,8,128]{1,3,2,0:T(8,128)S(1)}) fusion(f32[4,8,128]{2,1,0:T(8,128)S(1)} %bitcast.117, pred[4,8]{1,0:T(4,128)(4,1)S(1)} %iota_compare_fusion.5, bf16[4,8,128,256]{3,2,1,0:T(8,128)(2,1)S(1)} %bitcast.116, bf16[4,4,128,256]{3,2,1,0:T(8,128)(2,1)} %get-tuple-element.514, ...), kind=kOutput, calls=%fused_computation.11.clone.1 | convolution fusion | flops 270532096 | bytes 4475424 | tf_op jit(solution)/shard_map/while/body/eval_jaxpr/gbd,gscd->gbsc/dot_general | solution.py:68
  61.8 0.8 exponential_reduce_fusion.2
  63.3 0.7 gather_fusion.1
  64.1 1.9 %select_reduce_fusion.2 = (f32[4,128]{1,0:T(4,128)S(1)}, f32[4,128,8,128]{1,3,2,0:T(8,128)S(1)}) fusion(f32[4,8,128]{2,1,0:T(8,128)S(1)} %bitcast.117, pred[4,8]{1,0:T(4,128)(4,1)S(1)} %iota_compare_fusion.5, bf16[4,8,128,256]{3,2,1,0:T(8,128)(2,1)S(1)} %bitcast.116, bf16[4,4,128,256]{3,2,1,0:T(8,128)(2,1)} %get-tuple-element.514, ...), kind=kOutput, calls=%fused_computation.11.clone.1 | convolution fusion | flops 270532096 | bytes 4475424 | tf_op jit(solution)/shard_map/while/body/eval_jaxpr/gbd,gscd->gbsc/dot_general | solution.py:68
  66.0 0.8 exponential_reduce_fusion.2
  68.2 1.9 %select_reduce_fusion.2 = (f32[4,128]{1,0:T(4,128)S(1)}, f32[4,128,8,128]{1,3,2,0:T(8,128)S(1)}) fusion(f32[4,8,128]{2,1,0:T(8,128)S(1)} %bitcast.117, pred[4,8]{1,0:T(4,128)(4,1)S(1)} %iota_compare_fusion.5, bf16[4,8,128,256]{3,2,1,0:T(8,128)(2,1)S(1)} %bitcast.116, bf16[4,4,128,256]{3,2,1,0:T(8,128)(2,1)} %get-tuple-element.514, ...), kind=kOutput, calls=%fused_computation.11.clone.1 | convolution fusion | flops 270532096 | bytes 4475424 | tf_op jit(solution)/shard_map/while/body/eval_jaxpr/gbd,gscd->gbsc/dot_general | solution.py:68
  70.1 0.8 exponential_reduce_fusion.2
  70.9 5.2 %all-gather = f32[16,4,128]{2,1,0:T(4,128)S(1)} all-gather(f32[4,4,128]{2,1,0:T(4,128)S(1)} %get-tuple-element.235), channel_id=2, replica_groups=mesh['imp'=8,'camp'=4] {'camp'}, dimensions={0}, use_global_device_ids=true | all-gather | bytes 40960 | tf_op jit(solution)/shard_map/all_gather | solution.py:34
  76.1 5.2 %all-gather.1 = f32[16,4,128]{2,1,0:T(4,128)S(1)} all-gather(f32[4,4,128]{2,1,0:T(4,128)S(1)} %get-tuple-element.236), channel_id=3, replica_groups=mesh['imp'=8,'camp'=4] {'camp'}, dimensions={0}, use_global_device_ids=true | all-gather | bytes 40960 | tf_op jit(solution)/shard_map/all_gather | solution.py:34
  81.4 14.7 %while.42 = (s32[]{:T(128)}, f32[8,128]{1,0:T(8,128)S(1)}, s32[4,4,8]{2,1,0:T(4,128)S(1)}, s32[4,4]{1,0:T(4,128)S(1)}, bf16[4,4,128,256]{3,2,1,0:T(8,128)(2,1)},...) while((s32[]{:T(128)}, f32[8,128]{1,0:T(8,128)S(1)}, ...), condition=%wide.region_8.9_spmd.clone, body=%wide.region_6.8_spmd.clone.sunk | while | flops 272498304 | bytes 6668323 | solution.py:105
  81.5 0.7 gather_fusion.2
  82.9 2.0 %multiply_reduce_fusion.2 = f32[4,8,128]{2,1,0:T(8,128)S(1)} fusion(bf16[4,8,128,256]{3,2,1,0:T(8,128)(2,1)S(1)} %bitcast.115, f32[4,128]{1,0:T(4,128)S(1)} %get-tuple-element.490, f32[4,128]{1,0:T(4,128)S(1)} %get-tuple-element.491, f32[4,128]{1,0:T(4,128)S(1)} %dynamic-slice_bitcast_fusion.8, f32[4,8,128]{2,1,0:T(8,128)S(1)} %bitcast.121, ...), kind=kOutput, calls=%fused_computation.24.clone.1 | convolution fusion | flops 272101376 | bytes 2398752 | tf_op jit(solution)/shard_map/while/body/eval_jaxpr/gbd,gscd->gbsc/dot_general | solution.py:68
  85.2 0.7 gather_fusion.2
  86.6 2.0 %multiply_reduce_fusion.2 = f32[4,8,128]{2,1,0:T(8,128)S(1)} fusion(bf16[4,8,128,256]{3,2,1,0:T(8,128)(2,1)S(1)} %bitcast.115, f32[4,128]{1,0:T(4,128)S(1)} %get-tuple-element.490, f32[4,128]{1,0:T(4,128)S(1)} %get-tuple-element.491, f32[4,128]{1,0:T(4,128)S(1)} %dynamic-slice_bitcast_fusion.8, f32[4,8,128]{2,1,0:T(8,128)S(1)} %bitcast.121, ...), kind=kOutput, calls=%fused_computation.24.clone.1 | convolution fusion | flops 272101376 | bytes 2398752 | tf_op jit(solution)/shard_map/while/body/eval_jaxpr/gbd,gscd->gbsc/dot_general | solution.py:68
  88.9 0.7 gather_fusion.2
  90.3 2.0 %multiply_reduce_fusion.2 = f32[4,8,128]{2,1,0:T(8,128)S(1)} fusion(bf16[4,8,128,256]{3,2,1,0:T(8,128)(2,1)S(1)} %bitcast.115, f32[4,128]{1,0:T(4,128)S(1)} %get-tuple-element.490, f32[4,128]{1,0:T(4,128)S(1)} %get-tuple-element.491, f32[4,128]{1,0:T(4,128)S(1)} %dynamic-slice_bitcast_fusion.8, f32[4,8,128]{2,1,0:T(8,128)S(1)} %bitcast.121, ...), kind=kOutput, calls=%fused_computation.24.clone.1 | convolution fusion | flops 272101376 | bytes 2398752 | tf_op jit(solution)/shard_map/while/body/eval_jaxpr/gbd,gscd->gbsc/dot_general | solution.py:68
  92.6 0.7 gather_fusion.2
  94.0 2.0 %multiply_reduce_fusion.2 = f32[4,8,128]{2,1,0:T(8,128)S(1)} fusion(bf16[4,8,128,256]{3,2,1,0:T(8,128)(2,1)S(1)} %bitcast.115, f32[4,128]{1,0:T(4,128)S(1)} %get-tuple-element.490, f32[4,128]{1,0:T(4,128)S(1)} %get-tuple-element.491, f32[4,128]{1,0:T(4,128)S(1)} %dynamic-slice_bitcast_fusion.8, f32[4,8,128]{2,1,0:T(8,128)S(1)} %bitcast.121, ...), kind=kOutput, calls=%fused_computation.24.clone.1 | convolution fusion | flops 272101376 | bytes 2398752 | tf_op jit(solution)/shard_map/while/body/eval_jaxpr/gbd,gscd->gbsc/dot_general | solution.py:68
  96.2 20.3 %psum.7 = f32[1024]{0:T(1024)S(1)} all-reduce(f32[1024]{0:T(1024)S(1)} %bitcast.125), channel_id=1, replica_groups=mesh['imp'=8,'camp'=4] {'imp'}, use_global_device_ids=true, to_apply=%region_9.10 | all-reduce | flops 1024 | bytes 8192 | tf_op jit(solution)/shard_map/psum | solution.py:110
  (99 shorter events, 11.2 us)
Async XLA Ops:
  7.2 47.2 %all-gather.5.cloned.1.call-start = ((), (), s32[]{:S(2)}) async-start(), calls=%async_computation | async-start | bytes 1310720 | tf_op jit(solution)/shard_map/all_gather | solution.py:46
  7.9 35.9 %collective-permute-start = (bf16[1,128]{1,0:T(2,128)(2,1)}, bf16[1,128]{1,0:T(2,128)(2,1)S(1)}, u32[]{:S(2)}, u32[]{:S(2)}) collective-permute-start(bf16[1,128]{1,0:T(2,128)(2,1)} %bitcast.128), channel_id=1, source_target_pairs={{0,4},{4,0},{8,12},{12,8},{16,20},{20,16},{24,28},{28,24},{1,5},{5... | collective-permute-start | bytes 776 | tf_op jit(solution)/shard_map/ppermute | solution.py:22
  44.5 5.3 %collective-permute-start.1 = (bf16[2,128]{1,0:T(2,128)(2,1)S(1)}, bf16[2,128]{1,0:T(2,128)(2,1)S(1)}, u32[]{:S(2)}, u32[]{:S(2)}) collective-permute-start(bf16[2,128]{1,0:T(2,128)(2,1)S(1)} %pad_maximum_fusion.1), channel_id=1, source_target_pairs={{0,8},{4,12},{8,0},{12,4},{16,24},{20,28},{24,16},{28,20},{1,9},{5... | collective-permute-start | bytes 1544 | tf_op jit(solution)/shard_map/ppermute | solution.py:22
  49.8 4.5 %collective-permute-start.2 = (bf16[4,128]{1,0:T(4,128)(2,1)S(1)}, bf16[4,128]{1,0:T(4,128)(2,1)S(1)}, u32[]{:S(2)}, u32[]{:S(2)}) collective-permute-start(bf16[4,128]{1,0:T(4,128)(2,1)S(1)} %pad_maximum_fusion), channel_id=1, source_target_pairs={{0,16},{4,20},{8,24},{12,28},{16,0},{20,4},{24,8},{28,12},{1,17},{... | collective-permute-start | bytes 3080 | tf_op jit(solution)/shard_map/ppermute | solution.py:22
  81.4 35.7 %copy-start = (bf16[128]{0:T(256)(128)(2,1)S(1)}, bf16[128]{0:T(256)(128)(2,1)}, u32[]{:S(2)}) copy-start(bf16[128]{0:T(256)(128)(2,1)} %param.16) | copy-start | bytes 772
  81.4 35.7 %copy-start.1 = (f32[128]{0:T(128)S(1)}, f32[128]{0:T(128)}, u32[]{:S(2)}) copy-start(f32[128]{0:T(128)} %param.17) | copy-start | bytes 1540
Sparse Core Ops, SparseCore 0:
  9.5 19.4 all-gather.4
